TPU v7x, 512 devices: a whole 4x4x16 slice. The times are simulated.
512 devices in a mesh: seq: 64 (over z, x), head: 8 (over y, core).
Axes of the slice: x: 4, y: 4, z: 16, core: 2. Of those that a mesh axis runs over, the one named last changes fastest.
Arguments:
- queries: bfloat16 [16384, 8192], P(('seq', 'head')), may hold values from -6 to 6
- key_vectors: bfloat16 [16384, 8192], P(('seq', 'head')), may hold values from -6 to 6
- value_vectors: bfloat16 [16384, 8192], P(('seq', 'head')), may hold values from -6 to 6
- out_grad: bfloat16 [16384, 8192], P(('seq', 'head')), may hold values from -6 to 6
Outputs:
- query_grad: bfloat16 [16384, 8192], P(('seq', 'head'))
- key_grad: bfloat16 [16384, 8192], P(('seq', 'head'))
- value_grad: bfloat16 [16384, 8192], P(('seq', 'head'))
All inputs are finite; a program needn't handle non-finite values.
Results may differ from a plain program's by a relative error of at most 0.005.
Values may be sent and summed in bfloat16 or wider, within the bound.
No kernel may reach another device: no remote copies, remote signals or barrier semaphores. Data moves between devices by JAX's collectives and lax.ppermute only.
A program may use at most 192 MiB of HBM per device.

v0:
```python
import jax
import jax.numpy as jnp
from jax import lax
from jax.sharding import PartitionSpec as P

HEAD_DIM = 128


def carried_in(value, axis, combine, identity, reverse):
    peers, here = (lax.axis_size(axis), lax.axis_index(axis))
    everything = lax.all_gather(value, axis)
    start = jnp.broadcast_to(jnp.asarray(identity, value.dtype), value.shape)

    def turn(k, before):
        at = peers - 1 - k if reverse else k
        reached = at > here if reverse else at < here
        new = combine(before, everything[at])
        return jnp.where(reached, new, before)

    return lax.fori_loop(0, peers, turn, start)


def combine_sum(earlier, later):
    return jax.tree.map(jnp.add, earlier, later)


def local(queries, key_vectors, value_vectors, out_grad):
    f32 = jnp.float32
    hi = lax.Precision.HIGHEST
    groups = lax.axis_size("head")
    rows = queries.shape[0] * groups
    width = queries.shape[1] // groups
    heads = width // HEAD_DIM
    q_loc, k_loc, v_loc, g_loc = (
        lax.all_to_all(queries, "head", split_axis=1, concat_axis=0, tiled=True),
        lax.all_to_all(key_vectors, "head", split_axis=1, concat_axis=0, tiled=True),
        lax.all_to_all(value_vectors, "head", split_axis=1, concat_axis=0, tiled=True),
        lax.all_to_all(out_grad, "head", split_axis=1, concat_axis=0, tiled=True),
    )
    start = (lax.axis_index("seq") * rows).astype(f32)
    position = jnp.arange(rows, dtype=f32) + start
    factor = lax.rsqrt(HEAD_DIM * (position + 1.0))
    scaled = (g_loc.astype(f32) * factor[:, None]).astype(jnp.bfloat16)

    def head_major(x):
        return jnp.transpose(x.reshape(rows, heads, HEAD_DIM), (1, 0, 2))

    qh = head_major(q_loc)
    kh = head_major(k_loc)
    vh = head_major(v_loc)
    gh = head_major(scaled)
    kv_sum = jnp.einsum("htd,hte->hde", kh, vh, preferred_element_type=f32)
    qg_sum = jnp.einsum("htd,hte->hde", qh, gh, preferred_element_type=f32)
    zero_state = jnp.zeros((heads, HEAD_DIM, HEAD_DIM), f32)
    before = carried_in(kv_sum, "seq", combine_sum, zero_state, False)
    after = carried_in(qg_sum, "seq", combine_sum, zero_state, True)
    index = jnp.arange(rows, dtype=jnp.int32)
    keep = index[:, None] >= index[None, :]
    inner = jnp.where(
        keep[None], jnp.einsum("hte,hse->hts", gh, vh, preferred_element_type=f32), 0.0
    ).astype(jnp.bfloat16)
    pairs = jnp.where(
        keep[None], jnp.einsum("htd,hsd->hts", qh, kh, preferred_element_type=f32), 0.0
    ).astype(jnp.bfloat16)
    dq = jnp.einsum("hts,hsd->htd", inner, kh, preferred_element_type=f32) + jnp.einsum(
        "hte,hde->htd", gh.astype(f32), before, precision=hi
    )
    dk = jnp.einsum("hts,htd->hsd", inner, qh, preferred_element_type=f32) + jnp.einsum(
        "hse,hde->hsd", vh.astype(f32), after, precision=hi
    )
    dv = jnp.einsum("hts,hte->hse", pairs, gh, preferred_element_type=f32) + jnp.einsum(
        "hsd,hde->hse", kh.astype(f32), after, precision=hi
    )

    def token_major(x):
        return jnp.transpose(x.astype(jnp.bfloat16), (1, 0, 2)).reshape(rows, width)

    dq_loc = token_major(dq)
    dk_loc = token_major(dk)
    dv_loc = token_major(dv)
    query_grad, key_grad, value_grad = (
        lax.all_to_all(dq_loc, "head", split_axis=0, concat_axis=1, tiled=True),
        lax.all_to_all(dk_loc, "head", split_axis=0, concat_axis=1, tiled=True),
        lax.all_to_all(dv_loc, "head", split_axis=0, concat_axis=1, tiled=True),
    )
    return (query_grad, key_grad, value_grad)


def solution(mesh):
    placed = (
        P(("seq", "head"), None),
        P(("seq", "head"), None),
        P(("seq", "head"), None),
        P(("seq", "head"), None),
    )
    return jax.shard_map(
        local,
        mesh=mesh,
        in_specs=placed,
        out_specs=(P(("seq", "head"), None), P(("seq", "head"), None), P(("seq", "head"), None)),
        check_vma=False,
    )
```

profile of v0, /device:TPU:1, one launch (start us, length us, event | category | flops | bytes accessed | tf_op | source)
XLA Modules:
  0.0 733.2 jit_solution(7795061028266321221)
XLA Ops:
  7.2 1.9 copy.158
  9.1 10.2 %all-to-all-start = ((bf16[32,8,1024]{2,0,1:T(8,128)(2,1)}), bf16[32,8,1024]{2,0,1:T(8,128)(2,1)S(1)}, u32[]{:S(2)}, u32[]{:S(2)}) async-start(bf16[32,8,1024]{2,0,1:T(8,128)(2,1)} %bitcast.100), calls=%async_computation | async-start | bytes 1048576 | tf_op jit(solution)/shard_map/all_to_all | solution.py:38
  20.2 8.5 %all-to-all-done = bf16[32,8,1024]{2,0,1:T(8,128)(2,1)S(1)} async-done(((bf16[32,8,1024]{2,0,1:T(8,128)(2,1)}), bf16[32,8,1024]{2,0,1:T(8,128)(2,1)S(1)}, u32[]{:S(2)}, u32[]{:S(2)}) %all-to-all-start) | async-done | bytes 524320 | tf_op jit(solution)/shard_map/all_to_all | solution.py:38
  28.7 4.4 all-to-all-start.4
  33.4 9.0 %all-to-all-done.4 = bf16[32,8,1024]{2,0,1:T(8,128)(2,1)S(1)} async-done(((bf16[32,8,1024]{2,0,1:T(8,128)(2,1)}), bf16[32,8,1024]{2,0,1:T(8,128)(2,1)S(1)}, u32[]{:S(2)}, u32[]{:S(2)}) %all-to-all-start.4) | async-done | bytes 524320 | tf_op jit(solution)/shard_map/all_to_all | solution.py:35
  45.1 4.4 all-to-all-start.2
  50.3 8.5 %all-to-all-done.2 = bf16[32,8,1024]{2,0,1:T(8,128)(2,1)S(1)} async-done(((bf16[32,8,1024]{2,0,1:T(8,128)(2,1)}), bf16[32,8,1024]{2,0,1:T(8,128)(2,1)S(1)}, u32[]{:S(2)}, u32[]{:S(2)}) %all-to-all-start.2) | async-done | bytes 524320 | tf_op jit(solution)/shard_map/all_to_all | solution.py:36
  58.9 4.4 all-to-all-start.1
  63.4 9.3 %all-to-all-done.1 = bf16[32,8,1024]{2,0,1:T(8,128)(2,1)S(1)} async-done(((bf16[32,8,1024]{2,0,1:T(8,128)(2,1)}), bf16[32,8,1024]{2,0,1:T(8,128)(2,1)S(1)}, u32[]{:S(2)}, u32[]{:S(2)}) %all-to-all-start.1) | async-done | bytes 524320 | tf_op jit(solution)/shard_map/all_to_all | solution.py:37
  75.4 1.5 convolution_bitcast_fusion.2
  76.9 258.3 %all-gather.7.cloned.1.call-done = f32[512,128,128]{2,1,0:T(8,128)} async-done(((f32[8,128,128]{2,1,0:T(8,128)}), f32[512,128,128]{2,1,0:T(8,128)}) %all-gather.7.cloned.1.call-update) | async-done | bytes 33554448 | tf_op jit(solution)/shard_map/all_gather | solution.py:11
  335.2 80.6 %while.31 = (s32[]{:T(128)}, f32[8,128,128]{2,1,0:T(8,128)S(1)}, s32[]{:T(128)}, f32[64,8,128,128]{3,2,1,0:T(8,128)}, s32[]{:T(128)}, /*index=5*/s32[]{:T(128)}, s32[]{:T(128)}, s32[]{:T(128)}) while((s32[]{:T(128)}, f32[8,128,128]{2,1,0:T(8,128)S(1)}, s32[]{:T(128)}, f32[64,8,128,128]{3,2,1,0:T(8,128)}, s32[]{:T(128)}, ...), condition=%wide.region_3.4_spmd.clone, body=%wide.region_2.3_spmd.clone.sunk | while | flops 393224 | bytes 1573019 | solution.py:20
  356.6 1.2 add_select_fusion.5
  359.1 1.2 add_select_fusion.5
  360.4 1.2 add_select_fusion.5
  364.2 1.2 add_select_fusion.5
  378.1 1.2 add_select_fusion.5
  388.2 1.2 add_select_fusion.5
  392.0 1.2 add_select_fusion.5
  415.9 1.6 convolution_bitcast_fusion
  417.5 2.8 fusion.4
  420.2 1.4 copy.82
  422.6 5.9 all-to-all-start.6
  428.5 3.1 fusion.20
  433.5 4.4 all-to-all-done.6
  437.9 4.4 all-to-all-start.5
  442.3 186.0 %all-gather.5.cloned.1.call-done = f32[512,128,128]{2,1,0:T(8,128)} async-done(((f32[8,128,128]{2,1,0:T(8,128)}), f32[512,128,128]{2,1,0:T(8,128)}) %all-gather.5.cloned.1.call-update) | async-done | bytes 33554448 | tf_op jit(solution)/shard_map/all_gather | solution.py:11
  628.3 80.1 %while.30 = (s32[]{:T(128)}, f32[8,128,128]{2,1,0:T(8,128)S(1)}, s32[]{:T(128)}, f32[64,8,128,128]{3,2,1,0:T(8,128)}, s32[]{:T(128)}, /*index=5*/s32[]{:T(128)}) while((s32[]{:T(128)}, f32[8,128,128]{2,1,0:T(8,128)S(1)}, s32[]{:T(128)}, f32[64,8,128,128]{3,2,1,0:T(8,128)}, s32[]{:T(128)}, /*index=5*/s32[]{:T(128)}) %tuple.84), condition=%wide.region_1.2_spmd.clone, body=%wide.region_0.1_spmd.clone.sunk | while | flops 393220 | bytes 1572957 | solution.py:20
  628.3 1.3 add_select_fusion.4
  710.5 5.7 all-to-all-start.3
  716.1 1.9 copy.98
  718.8 6.6 all-to-all-done.3
  (163 shorter events, 161.4 us)
Async XLA Ops:
  7.2 12.2 %copy-start.3 = (bf16[32,8192]{1,0:T(8,128)(2,1)S(1)}, bf16[32,8192]{1,0:T(8,128)(2,1)}, u32[]{:S(2)}) copy-start(bf16[32,8192]{1,0:T(8,128)(2,1)} %param.8) | copy-start | bytes 1572868
  9.1 19.6 %all-to-all-start = ((bf16[32,8,1024]{2,0,1:T(8,128)(2,1)}), bf16[32,8,1024]{2,0,1:T(8,128)(2,1)S(1)}, u32[]{:S(2)}, u32[]{:S(2)}) async-start(bf16[32,8,1024]{2,0,1:T(8,128)(2,1)} %bitcast.100), calls=%async_computation | async-start | bytes 1048576 | tf_op jit(solution)/shard_map/all_to_all | solution.py:38
  28.7 13.7 %all-to-all-start.4 = ((bf16[32,8,1024]{2,0,1:T(8,128)(2,1)}), bf16[32,8,1024]{2,0,1:T(8,128)(2,1)S(1)}, u32[]{:S(2)}, u32[]{:S(2)}) async-start(bf16[32,8,1024]{2,0,1:T(8,128)(2,1)} %bitcast.97), calls=%async_computation.4 | async-start | bytes 1048576 | tf_op jit(solution)/shard_map/all_to_all | solution.py:35
  33.1 302.2 %all-gather.7.cloned.1.call-start = ((), (), s32[]{:S(2)}) async-start(), calls=%async_computation.8 | async-start | bytes 34078720 | tf_op jit(solution)/shard_map/all_gather | solution.py:11
  42.6 1.7 copy-start.4
  43.3 6.2 copy-start.5
  45.1 13.7 %all-to-all-start.2 = ((bf16[32,8,1024]{2,0,1:T(8,128)(2,1)}), bf16[32,8,1024]{2,0,1:T(8,128)(2,1)S(1)}, u32[]{:S(2)}, u32[]{:S(2)}) async-start(bf16[32,8,1024]{2,0,1:T(8,128)(2,1)} %bitcast.98), calls=%async_computation.2 | async-start | bytes 1048576 | tf_op jit(solution)/shard_map/all_to_all | solution.py:36
  58.9 13.7 %all-to-all-start.1 = ((bf16[32,8,1024]{2,0,1:T(8,128)(2,1)}), bf16[32,8,1024]{2,0,1:T(8,128)(2,1)S(1)}, u32[]{:S(2)}, u32[]{:S(2)}) async-start(bf16[32,8,1024]{2,0,1:T(8,128)(2,1)} %bitcast.99), calls=%async_computation.1 | async-start | bytes 1048576 | tf_op jit(solution)/shard_map/all_to_all | solution.py:37
  63.2 565.1 %all-gather.5.cloned.1.call-start = ((), (), s32[]{:S(2)}) async-start(), calls=%async_computation.7 | async-start | bytes 34078720 | tf_op jit(solution)/shard_map/all_gather | solution.py:11
  74.4 1.0 copy-start.1
  422.6 15.3 %all-to-all-start.6 = ((bf16[8,32,1024]{2,1,0:T(8,128)(2,1)}), bf16[8,32,1024]{2,1,0:T(8,128)(2,1)}, u32[]{:S(2)}, u32[]{:S(2)}) async-start(bf16[8,32,1024]{2,1,0:T(8,128)(2,1)} %all_to_all.107), calls=%async_computation.6 | async-start | bytes 1048576 | tf_op jit(solution)/shard_map/all_to_all | solution.py:84
  428.5 3.1 copy-start
  437.9 272.5 %all-to-all-start.5 = ((bf16[8,32,1024]{2,1,0:T(8,128)(2,1)}), bf16[8,32,1024]{2,1,0:T(8,128)(2,1)S(1)}, u32[]{:S(2)}, u32[]{:S(2)}) async-start(bf16[8,32,1024]{2,1,0:T(8,128)(2,1)} %all_to_all.103), calls=%async_computation.5 | async-start | bytes 1048576 | tf_op jit(solution)/shard_map/all_to_all | solution.py:83
  628.3 80.1 %copy-start.2 = (f32[8,256,128]{2,1,0:T(8,128)S(1)}, f32[8,256,128]{2,1,0:T(8,128)}, u32[]{:S(2)}) copy-start(f32[8,256,128]{2,1,0:T(8,128)} %fusion.20) | copy-start | bytes 3145732
  710.5 15.0 %all-to-all-start.3 = ((bf16[8,32,1024]{2,1,0:T(8,128)(2,1)}), bf16[8,32,1024]{2,1,0:T(8,128)(2,1)S(1)}, u32[]{:S(2)}, u32[]{:S(2)}) async-start(bf16[8,32,1024]{2,1,0:T(8,128)(2,1)} %all_to_all.96), calls=%async_computation.3 | async-start | bytes 1048576 | tf_op jit(solution)/shard_map/all_to_all | solution.py:82
Sparse Core Ops, SparseCore 0:
  44.4 290.7 all-gather.6
  338.8 289.5 all-gather.4
where the time goes:
time: 740 us; the launch traced here: 733 us
  waiting for transfers between devices  491 us (66%)
  other arithmetic  158 us (21%)
  starting transfers between devices  39.2 us (5%)
  local copies, waits for them, and re-layouts  15.6 us (2%)
  between operations  14.2 us (2%)
  matrix products  12 us (2%)
    all_gather x2, waiting for transfers between devices, carried_in(): everything = lax.all_gather(value, axis)  444 us
    select_n x128, other arithmetic, turn(): return jnp.where(reached, new, before)  157 us
  transfers between devices with their start and end apart: 9, of which 8 were waited for; matrix products, arithmetic and copies ran while one was open for 24% of the time, Pallas kernels for 0%

commit v1 on v0

--- a/solution.py
+++ b/solution.py
@@ -35,7 +35,15 @@
         lax.all_to_all(queries, "head", split_axis=1, concat_axis=0, tiled=True),
         lax.all_to_all(key_vectors, "head", split_axis=1, concat_axis=0, tiled=True),
         lax.all_to_all(value_vectors, "head", split_axis=1, concat_axis=0, tiled=True),
-        lax.all_to_all(out_grad, "head", split_axis=1, concat_axis=0, tiled=True),
+        jnp.concatenate(
+            lax.all_to_all(
+                jnp.stack(jnp.split(out_grad, lax.axis_size("head"), axis=1), axis=0),
+                axis_name="head",
+                split_axis=0,
+                concat_axis=0,
+            ),
+            axis=0,
+        ),
     )
     start = (lax.axis_index("seq") * rows).astype(f32)
     position = jnp.arange(rows, dtype=f32) + start

time: 740 us -> 750 us (1.014)
  local copies, waits for them, and re-layouts: 15.6 us -> 24.4 us
    unnamed x16 -> x23, local copies, waits for them, and re-layouts: 1.5 us -> 11.8 us
where the time goes in v1:
time: 750 us; the launch traced here: 743 us
  waiting for transfers between devices  492 us (66%)
  other arithmetic  158 us (21%)
  starting transfers between devices  39.2 us (5%)
  local copies, waits for them, and re-layouts  24.4 us (3%)
  between operations  14.2 us (2%)
  matrix products  12 us (2%)
    all_gather x2, waiting for transfers between devices, carried_in(): everything = lax.all_gather(value, axis)  444 us
    select_n x128, other arithmetic, turn(): return jnp.where(reached, new, before)  157 us
  transfers between devices with their start and end apart: 9, of which 8 were waited for; matrix products, arithmetic and copies ran while one was open for 24% of the time, Pallas kernels for 0%

profile of v1, /device:TPU:1, one launch (start us, length us, event | category | flops | bytes accessed | tf_op | source)
XLA Modules:
  0.0 743.0 jit_solution(14074551777151623834)
XLA Ops:
  7.2 1.5 bitcast_dynamic-update-slice_fusion.7
  8.7 1.5 bitcast_dynamic-update-slice_fusion.6
  10.2 1.5 bitcast_dynamic-update-slice_fusion.5
  11.7 1.5 bitcast_dynamic-update-slice_fusion.4
  13.1 1.5 bitcast_dynamic-update-slice_fusion.3
  14.6 1.5 bitcast_dynamic-update-slice_fusion.2
  16.1 1.5 bitcast_dynamic-update-slice_fusion.1
  17.5 1.5 bitcast_dynamic-update-slice_fusion
  19.0 10.2 %all-to-all-start = ((bf16[8,32,1024]{2,1,0:T(8,128)(2,1)}), bf16[8,32,1024]{2,1,0:T(8,128)(2,1)S(1)}, u32[]{:S(2)}, u32[]{:S(2)}) async-start(bf16[8,32,1024]{2,1,0:T(8,128)(2,1)} %bitcast_dynamic-update-slice_fusion), calls=%async_computation | async-start | bytes 1048576 | tf_op jit(solution)/shard_map/all_to_all | solution.py:39
  30.1 8.5 %all-to-all-done = bf16[8,32,1024]{2,1,0:T(8,128)(2,1)S(1)} async-done(((bf16[8,32,1024]{2,1,0:T(8,128)(2,1)}), bf16[8,32,1024]{2,1,0:T(8,128)(2,1)S(1)}, u32[]{:S(2)}, u32[]{:S(2)}) %all-to-all-start) | async-done | bytes 524320 | tf_op jit(solution)/shard_map/all_to_all | solution.py:39
  38.6 4.4 all-to-all-start.4
  43.1 9.2 %all-to-all-done.4 = bf16[32,8,1024]{2,0,1:T(8,128)(2,1)S(1)} async-done(((bf16[32,8,1024]{2,0,1:T(8,128)(2,1)}), bf16[32,8,1024]{2,0,1:T(8,128)(2,1)S(1)}, u32[]{:S(2)}, u32[]{:S(2)}) %all-to-all-start.4) | async-done | bytes 524320 | tf_op jit(solution)/shard_map/all_to_all | solution.py:35
  55.0 4.4 all-to-all-start.2
  60.2 8.5 %all-to-all-done.2 = bf16[32,8,1024]{2,0,1:T(8,128)(2,1)S(1)} async-done(((bf16[32,8,1024]{2,0,1:T(8,128)(2,1)}), bf16[32,8,1024]{2,0,1:T(8,128)(2,1)S(1)}, u32[]{:S(2)}, u32[]{:S(2)}) %all-to-all-start.2) | async-done | bytes 524320 | tf_op jit(solution)/shard_map/all_to_all | solution.py:36
  68.7 4.4 all-to-all-start.1
  73.2 9.3 %all-to-all-done.1 = bf16[32,8,1024]{2,0,1:T(8,128)(2,1)S(1)} async-done(((bf16[32,8,1024]{2,0,1:T(8,128)(2,1)}), bf16[32,8,1024]{2,0,1:T(8,128)(2,1)S(1)}, u32[]{:S(2)}, u32[]{:S(2)}) %all-to-all-start.1) | async-done | bytes 524320 | tf_op jit(solution)/shard_map/all_to_all | solution.py:37
  85.3 1.5 convolution_bitcast_fusion.2
  86.7 258.4 %all-gather.7.cloned.1.call-done = f32[512,128,128]{2,1,0:T(8,128)} async-done(((f32[8,128,128]{2,1,0:T(8,128)}), f32[512,128,128]{2,1,0:T(8,128)}) %all-gather.7.cloned.1.call-update) | async-done | bytes 33554448 | tf_op jit(solution)/shard_map/all_gather | solution.py:11
  345.1 80.6 %while.31 = (s32[]{:T(128)}, f32[8,128,128]{2,1,0:T(8,128)S(1)}, s32[]{:T(128)}, f32[64,8,128,128]{3,2,1,0:T(8,128)}, s32[]{:T(128)}, /*index=5*/s32[]{:T(128)}, s32[]{:T(128)}, s32[]{:T(128)}) while((s32[]{:T(128)}, f32[8,128,128]{2,1,0:T(8,128)S(1)}, s32[]{:T(128)}, f32[64,8,128,128]{3,2,1,0:T(8,128)}, s32[]{:T(128)}, ...), condition=%wide.region_3.4_spmd.clone, body=%wide.region_2.3_spmd.clone.sunk | while | flops 393224 | bytes 1573019 | solution.py:20
  369.0 1.2 add_select_fusion.5
  425.7 1.6 convolution_bitcast_fusion
  427.3 2.7 fusion.4
  430.1 1.4 copy.74
  432.5 5.9 all-to-all-start.6
  438.3 3.0 fusion.21
  443.3 4.3 all-to-all-done.6
  447.7 4.4 all-to-all-start.5
  452.0 186.1 %all-gather.5.cloned.1.call-done = f32[512,128,128]{2,1,0:T(8,128)} async-done(((f32[8,128,128]{2,1,0:T(8,128)}), f32[512,128,128]{2,1,0:T(8,128)}) %all-gather.5.cloned.1.call-update) | async-done | bytes 33554448 | tf_op jit(solution)/shard_map/all_gather | solution.py:11
  638.2 80.1 %while.30 = (s32[]{:T(128)}, f32[8,128,128]{2,1,0:T(8,128)S(1)}, s32[]{:T(128)}, f32[64,8,128,128]{3,2,1,0:T(8,128)}, s32[]{:T(128)}, /*index=5*/s32[]{:T(128)}) while((s32[]{:T(128)}, f32[8,128,128]{2,1,0:T(8,128)S(1)}, s32[]{:T(128)}, f32[64,8,128,128]{3,2,1,0:T(8,128)}, s32[]{:T(128)}, /*index=5*/s32[]{:T(128)}) %tuple.84), condition=%wide.region_1.2_spmd.clone, body=%wide.region_0.1_spmd.clone.sunk | while | flops 393220 | bytes 1572957 | solution.py:20
  638.2 1.3 add_select_fusion.4
  720.3 5.7 all-to-all-start.3
  727.6 7.7 %all-to-all-done.3 = bf16[8,32,1024]{2,1,0:T(8,128)(2,1)S(1)} async-done(((bf16[8,32,1024]{2,1,0:T(8,128)(2,1)}), bf16[8,32,1024]{2,1,0:T(8,128)(2,1)S(1)}, u32[]{:S(2)}, u32[]{:S(2)}) %all-to-all-start.3) | async-done | bytes 524320 | tf_op jit(solution)/shard_map/all_to_all | solution.py:90
  (169 shorter events, 169.4 us)
Async XLA Ops:
  7.2 22.1 %copy-start.3 = (bf16[32,8192]{1,0:T(8,128)(2,1)S(1)}, bf16[32,8192]{1,0:T(8,128)(2,1)}, u32[]{:S(2)}) copy-start(bf16[32,8192]{1,0:T(8,128)(2,1)} %param.8) | copy-start | bytes 1572868
  19.0 19.6 %all-to-all-start = ((bf16[8,32,1024]{2,1,0:T(8,128)(2,1)}), bf16[8,32,1024]{2,1,0:T(8,128)(2,1)S(1)}, u32[]{:S(2)}, u32[]{:S(2)}) async-start(bf16[8,32,1024]{2,1,0:T(8,128)(2,1)} %bitcast_dynamic-update-slice_fusion), calls=%async_computation | async-start | bytes 1048576 | tf_op jit(solution)/shard_map/all_to_all | solution.py:39
  38.6 13.7 %all-to-all-start.4 = ((bf16[32,8,1024]{2,0,1:T(8,128)(2,1)}), bf16[32,8,1024]{2,0,1:T(8,128)(2,1)S(1)}, u32[]{:S(2)}, u32[]{:S(2)}) async-start(bf16[32,8,1024]{2,0,1:T(8,128)(2,1)} %bitcast.112), calls=%async_computation.4 | async-start | bytes 1048576 | tf_op jit(solution)/shard_map/all_to_all | solution.py:35
  43.0 302.1 %all-gather.7.cloned.1.call-start = ((), (), s32[]{:S(2)}) async-start(), calls=%async_computation.8 | async-start | bytes 34078720 | tf_op jit(solution)/shard_map/all_gather | solution.py:11
  52.5 1.7 copy-start.4
  53.1 6.2 copy-start.5
  55.0 13.7 %all-to-all-start.2 = ((bf16[32,8,1024]{2,0,1:T(8,128)(2,1)}), bf16[32,8,1024]{2,0,1:T(8,128)(2,1)S(1)}, u32[]{:S(2)}, u32[]{:S(2)}) async-start(bf16[32,8,1024]{2,0,1:T(8,128)(2,1)} %bitcast.113), calls=%async_computation.2 | async-start | bytes 1048576 | tf_op jit(solution)/shard_map/all_to_all | solution.py:36
  68.7 13.7 %all-to-all-start.1 = ((bf16[32,8,1024]{2,0,1:T(8,128)(2,1)}), bf16[32,8,1024]{2,0,1:T(8,128)(2,1)S(1)}, u32[]{:S(2)}, u32[]{:S(2)}) async-start(bf16[32,8,1024]{2,0,1:T(8,128)(2,1)} %bitcast.114), calls=%async_computation.1 | async-start | bytes 1048576 | tf_op jit(solution)/shard_map/all_to_all | solution.py:37
  73.1 565.1 %all-gather.5.cloned.1.call-start = ((), (), s32[]{:S(2)}) async-start(), calls=%async_computation.7 | async-start | bytes 34078720 | tf_op jit(solution)/shard_map/all_gather | solution.py:11
  84.3 1.0 copy-start.1
  432.5 15.2 %all-to-all-start.6 = ((bf16[8,32,1024]{2,1,0:T(8,128)(2,1)}), bf16[8,32,1024]{2,1,0:T(8,128)(2,1)S(1)}, u32[]{:S(2)}, u32[]{:S(2)}) async-start(bf16[8,32,1024]{2,1,0:T(8,128)(2,1)} %all_to_all.99), calls=%async_computation.6 | async-start | bytes 1048576 | tf_op jit(solution)/shard_map/all_to_all | solution.py:92
  438.3 3.0 copy-start
  447.7 272.6 %all-to-all-start.5 = ((bf16[8,32,1024]{2,1,0:T(8,128)(2,1)}), bf16[8,32,1024]{2,1,0:T(8,128)(2,1)S(1)}, u32[]{:S(2)}, u32[]{:S(2)}) async-start(bf16[8,32,1024]{2,1,0:T(8,128)(2,1)} %all_to_all.95), calls=%async_computation.5 | async-start | bytes 1048576 | tf_op jit(solution)/shard_map/all_to_all | solution.py:91
  638.2 80.1 %copy-start.2 = (f32[8,256,128]{2,1,0:T(8,128)S(1)}, f32[8,256,128]{2,1,0:T(8,128)}, u32[]{:S(2)}) copy-start(f32[8,256,128]{2,1,0:T(8,128)} %fusion.21) | copy-start | bytes 3145732
  720.3 15.0 %all-to-all-start.3 = ((bf16[8,32,1024]{2,1,0:T(8,128)(2,1)}), bf16[8,32,1024]{2,1,0:T(8,128)(2,1)S(1)}, u32[]{:S(2)}, u32[]{:S(2)}) async-start(bf16[8,32,1024]{2,1,0:T(8,128)(2,1)} %all_to_all.88), calls=%async_computation.3 | async-start | bytes 1048576 | tf_op jit(solution)/shard_map/all_to_all | solution.py:90
Sparse Core Ops, SparseCore 0:
  54.3 290.7 all-gather.6
  348.6 289.5 all-gather.4
